TPU v7x, 256 devices: a whole 4x4x8 slice. The times are simulated.
256 devices in a mesh: grp: 8 (over z), sub: 32 (over x, y, core).
Axes of the slice: x: 4, y: 4, z: 8, core: 2. Of those that a mesh axis runs over, the one named last changes fastest.
Arguments:
- residual: float32 [16, 98304], P(None, 'sub'), may hold values from -6 to 6
- margin: int32 [32, 8], replicated, may hold values from 0 to 767, as said below
- aggregate: int32 [768], P('sub'), may hold values from 0 to 63
- local_factor: bfloat16 [32, 4096, 4096], P('sub', 'grp'), may hold values from -0.09375 to 0.09375
- coarse_factor: bfloat16 [8192, 8192], P('sub'), may hold values from -0.0625 to 0.0625
Outputs:
- preconditioned: float32 [16, 98304], P('grp', 'sub')
Inputs may be any that keep to these rules, and one draw needn't show every extreme that they name: `margin`: for subdomain s, every entry names a block owned by another subdomain (block b is owned by subdomain b // 24); the entries of one row are distinct. Up to 8 entries of one row may name blocks of the same owner, and in every draw some row takes all of its entries from a single owner. `aggregate`: the counts of global blocks for each coarse block are whole numbers and may cross devices as int32.
All inputs are finite; a program needn't handle non-finite values.
Results may differ from a plain program's by a relative error of at most 0.0033.
Values sent between devices are 32-bit elements; how exact they have to be, the bound alone decides.
A program may use at most 64 MiB of HBM per device.

v0:
```python
import jax
import jax.numpy as jnp
from jax import lax
from jax.sharding import PartitionSpec as P

BLK = 128
NCB = 64


def row_of(table, index):
    return lax.dynamic_index_in_dim(table, index, 0, keepdims=False)


def on_device(residual, margin, aggregate, local_factor, coarse_factor):
    sub_count = lax.axis_size("sub")
    grp_count = lax.axis_size("grp")
    my_index = lax.axis_index("sub")
    grp_index = lax.axis_index("grp")
    rhs_count, own_width = residual.shape
    owned = own_width // BLK
    group_rows = rhs_count // grp_count
    blocks = residual.reshape(rhs_count, owned, BLK)
    exact = lax.Precision.HIGHEST
    my_list = row_of(margin, my_index)
    all_blocks = jnp.arange(owned * sub_count, dtype=jnp.int32)
    selector = (my_list[:, None] == all_blocks[None, :]).astype(jnp.float32)
    whole = lax.all_gather(blocks, "sub", axis=1, tiled=True)
    halo_rows = jnp.einsum("kb,rbc->rkc", selector, whole, precision=exact)
    local_rhs = (
        jnp.concatenate([blocks, halo_rows], axis=1).reshape(rhs_count, -1).astype(jnp.bfloat16)
    )
    factor = local_factor[0]
    inner_term = jnp.dot(local_rhs, factor.T, preferred_element_type=jnp.float32).astype(
        jnp.bfloat16
    )
    local_sol = lax.psum_scatter(
        jnp.dot(inner_term, factor, preferred_element_type=jnp.float32),
        "grp",
        scatter_dimension=0,
        tiled=True,
    )
    local_sol = local_sol.reshape(group_rows, -1, BLK)
    own_part = local_sol[:, :owned]
    back_rows = local_sol[:, owned:]
    spread = jnp.einsum("kb,rkc->rbc", selector, back_rows, precision=exact)
    returned = lax.psum_scatter(spread, "sub", scatter_dimension=1, tiled=True)
    catalog = jnp.arange(NCB, dtype=jnp.int32)
    member = (aggregate[:, None] == catalog[None, :]).astype(jnp.float32)
    mine = lax.dynamic_slice_in_dim(blocks, grp_index * group_rows, group_rows, 0)
    sums_part = jnp.einsum("rbk,bj->rjk", mine, member, precision=exact)
    sums, counts = lax.psum((sums_part, jnp.sum(member, axis=0)), "sub")
    coarse_rhs = (
        (sums / jnp.maximum(counts, 1.0)[None, :, None])
        .reshape(group_rows, -1)
        .astype(jnp.bfloat16)
    )
    inner_coarse = jnp.dot(coarse_rhs, coarse_factor.T, preferred_element_type=jnp.float32).astype(
        jnp.bfloat16
    )
    coarse_part = jnp.dot(inner_coarse, coarse_factor, preferred_element_type=jnp.float32)
    coarse_sol = lax.psum(coarse_part, "sub")
    prolonged = jnp.einsum(
        "rjk,bj->rbk", coarse_sol.reshape(group_rows, NCB, BLK), member, precision=exact
    )
    result = own_part + returned + prolonged
    return result.reshape(group_rows, -1)


def solution(mesh):
    placed = (P(None, "sub"), P(), P("sub"), P("sub", "grp", None), P("sub", None))
    return jax.shard_map(
        on_device, mesh=mesh, in_specs=placed, out_specs=P("grp", "sub"), check_vma=False
    )
```

profile of v0, /device:TPU:2, one launch (start us, length us, event | category | flops | bytes accessed | tf_op | source)
XLA Modules:
  0.0 460.0 jit_solution(2734043562929597561)
XLA Ops:
  6.5 0.0 copy-start
  6.5 0.0 all-reduce.5.cloned.1.call-start
  6.5 1.0 copy.9
  7.5 0.0 copy-start.1
  7.5 1.6 convolution_bitcast_fusion.2
  9.1 0.0 all-reduce.5.cloned.1.call-update
  9.2 0.0 all-gather.2.cloned.1.call-start
  9.2 0.0 copy-done.1
  9.2 0.7 all-gather.2.cloned.1.call-update
  9.9 0.0 all-reduce.9.cloned.1.call-start
  10.0 0.0 copy-done
  10.0 0.2 dynamic-slice_reduce_fusion
  10.2 1.3 dynamic-slice
  12.1 0.7 convert_reduce_fusion
  12.8 55.4 %psum.22 = f32[64]{0:T(128)S(1)} all-reduce(f32[64]{0:T(128)S(1)} %convert_reduce_fusion), channel_id=1, replica_groups=mesh['grp'=8,'sub'=32] {'sub'}, use_global_device_ids=true, to_apply=%region_4.5 | all-reduce | flops 64 | bytes 512 | tf_op jit(solution)/shard_map/psum | solution.py:51
  68.3 0.9 bitcast_convert_fusion
  69.2 50.8 %all-reduce.5.cloned.1.call-done = f32[2,64,128]{2,1,0:T(8,128)} async-done(((f32[2,64,128]{2,1,0:T(8,128)}), f32[2,64,128]{2,1,0:T(8,128)}) %all-reduce.5.cloned.1.call-update) | async-done | bytes 65552 | tf_op jit(solution)/shard_map/psum | solution.py:51
  120.0 0.9 fusion.20
  120.9 54.7 %all-gather.2.cloned.1.call-done = f32[16,768,128]{2,1,0:T(8,128)} async-done(((f32[16,24,128]{2,1,0:T(8,128)}), f32[16,768,128]{2,1,0:T(8,128)}) %all-gather.2.cloned.1.call-update) | async-done | bytes 6291472 | tf_op jit(solution)/shard_map/all_gather | solution.py:27
  175.7 4.8 %fusion.4 = bf16[16,8,128]{2,1,0:T(8,128)(2,1)S(1)} fusion(f32[16,768,128]{2,1,0:T(8,128)} %all-gather.2.cloned.1.call-done, s32[8]{0:T(128)S(1)} %dynamic-slice_reduce_fusion), kind=kOutput, calls=%fused_computation.8 | convolution fusion | flops 151017472 | bytes 6324256 | tf_op jit(solution)/shard_map/kb,rbc->rkc/dot_general | solution.py:28
  180.5 6.0 %fusion = f32[16,4096]{1,0:T(8,128)} fusion(bf16[1,512,4096]{2,1,0:T(8,128)(2,1)} %param.8, bf16[2,8,32,128]{3,2,1,0:T(8,128)(2,1)S(1)} %bitcast.65), kind=kOutput, calls=%fused_computation | convolution fusion | flops 134225920 | bytes 4587520 | tf_op jit(solution)/shard_map/dot_general | solution.py:37
  186.5 0.0 all-reduce.9.cloned.1.call-update
  186.5 0.0 copy-start.2
  186.6 0.0 all-reduce.7.cloned.1.call-start
  186.6 6.4 %convolution_bitcast_fusion.1 = f32[1,2,64,128]{3,1,2,0:T(2,128)S(1)} fusion(bf16[256,8192]{1,0:T(8,128)(2,1)} %param.9, bf16[1,2,64,128]{3,2,1,0:T(8,128)(2,1)S(1)} %fusion.20), kind=kOutput, calls=%fused_computation.5 | convolution fusion | flops 16777728 | bytes 4292608 | tf_op jit(solution)/shard_map/dot_general | solution.py:60
  193.0 0.6 copy.28
  193.6 0.0 all-reduce.7.cloned.1.call-update
  193.6 0.0 reduce-scatter.2.cloned.1.call-start
  193.7 65.8 %all-reduce.9.cloned.1.call-done = f32[16,4096]{1,0:T(8,128)} async-done(((f32[16,4096]{1,0:T(8,128)}), f32[16,4096]{1,0:T(8,128)}) %all-reduce.9.cloned.1.call-update) | async-done | bytes 262160
  259.4 0.9 dynamic-slice_bitcast_fusion
  260.4 1.5 convolution_bitcast_fusion
  261.8 0.0 reduce-scatter.2.cloned.1.call-update
  261.9 105.6 %all-reduce.7.cloned.1.call-done = f32[2,64,128]{2,1,0:T(8,128)} async-done(((f32[2,64,128]{2,1,0:T(8,128)}), f32[2,64,128]{2,1,0:T(8,128)}) %all-reduce.7.cloned.1.call-update) | async-done | bytes 65552 | tf_op jit(solution)/shard_map/psum | solution.py:61
  367.4 84.3 %reduce-scatter.2.cloned.1.call-done = f32[2,24,128]{2,1,0:T(8,128)} async-done(((f32[2,768,128]{2,1,0:T(8,128)}), f32[2,24,128]{2,1,0:T(8,128)}) %reduce-scatter.2.cloned.1.call-update) | async-done | bytes 24592 | tf_op jit(solution)/shard_map/reduce_scatter | solution.py:46
  451.8 0.0 copy-done.2
  451.8 1.0 fusion.11
  452.8 0.6 copy.30
  (3 shorter events, 0.0 us)
Async XLA Ops:
  6.5 3.5 copy-start
  6.5 113.4 %all-reduce.5.cloned.1.call-start = ((), (), s32[]{:S(2)}) async-start(), calls=%async_computation.3 | async-start | bytes 131072 | tf_op jit(solution)/shard_map/psum | solution.py:51
  7.5 1.7 copy-start.1
  9.2 166.5 %all-gather.2.cloned.1.call-start = ((), (), s32[]{:S(2)}) async-start(), calls=%async_computation.1 | async-start | bytes 6488064 | tf_op jit(solution)/shard_map/all_gather | solution.py:27
  9.9 249.5 %all-reduce.9.cloned.1.call-start = ((), (), s32[]{:S(2)}) async-start(), calls=%async_computation.5 | async-start | bytes 524288
  186.5 265.2 %copy-start.2 = (s32[24]{0:T(128)S(1)}, s32[24]{0:T(128)}, u32[]{:S(2)}) copy-start(s32[24]{0:T(128)} %param.7) | copy-start | bytes 292
  186.6 180.9 %all-reduce.7.cloned.1.call-start = ((), (), s32[]{:S(2)}) async-start(), calls=%async_computation.4 | async-start | bytes 131072 | tf_op jit(solution)/shard_map/psum | solution.py:61
  193.6 258.1 %reduce-scatter.2.cloned.1.call-start = ((), (), s32[]{:S(2)}) async-start(), calls=%async_computation.2 | async-start | bytes 811008 | tf_op jit(solution)/shard_map/reduce_scatter | solution.py:46
Sparse Core Ops, SparseCore 0:
  10.6 109.3 all-reduce.4
  122.7 52.9 all-gather.1
  186.7 72.7 all-reduce.8
  262.5 104.8 all-reduce.6
  371.1 80.6 reduce-scatter.1
where the time goes:
time: 460 us
  waiting for transfers between devices  362 us (79%)
  blocking collectives  55.4 us (12%)
  matrix products  21.3 us (5%)
  between operations  13.9 us (3%)
  local copies, waits for them, and re-layouts  4.62 us (1%)
    psum x1, waiting for transfers between devices, on_device(): coarse_sol = lax.psum(coarse_part, 'sub')  106 us
    reduce_scatter x1, waiting for transfers between devices, on_device(): returned = lax.psum_scatter(spread, 'sub', scatter_dimension=1, tiled=True)  84.3 us
    unnamed x6, waiting for transfers between devices  66.5 us
    psum x1, blocking collectives, on_device(): sums, counts = lax.psum((sums_part, jnp.sum(member, axis=0)), 'sub')  55.4 us
    all_gather x1, waiting for transfers between devices, on_device(): whole = lax.all_gather(blocks, 'sub', axis=1, tiled=True)  54.7 us
    psum x1, waiting for transfers between devices, on_device(): sums, counts = lax.psum((sums_part, jnp.sum(member, axis=0)), 'sub')  50.8 us
  transfers between devices with their start and end apart: 5, of which 5 were waited for; matrix products, arithmetic and copies ran while one was open for 3% of the time, Pallas kernels for 0%

commit v1 on v0

--- a/solution.py
+++ b/solution.py
@@ -58,7 +58,7 @@
         jnp.bfloat16
     )
     coarse_part = jnp.dot(inner_coarse, coarse_factor, preferred_element_type=jnp.float32)
-    coarse_sol = lax.psum(coarse_part, "sub")
+    coarse_sol = jnp.sum(lax.all_gather(coarse_part, "sub"), axis=0)
     prolonged = jnp.einsum(
         "rjk,bj->rbk", coarse_sol.reshape(group_rows, NCB, BLK), member, precision=exact
     )

time: 460 us -> 402 us (0.87)
  waiting for transfers between devices: 362 us -> 302 us
    psum x1 -> x0, waiting for transfers between devices: 106 us -> none  [on_device(): coarse_sol = lax.psum(coarse_part, 'sub')]
    all_gather x0 -> x1, waiting for transfers between devices: none -> 46.7 us  [on_device(): coarse_sol = jnp.sum(lax.all_gather(coarse_part, 'sub'), axis=0)]
  transfers between devices with their start and end apart: 5 -> 5, of which waited for: 5 -> 5; matrix products, arithmetic and copies ran while one was open for 3% -> 4% of each run, Pallas kernels for 0% -> 0%
where the time goes in v1:
time: 402 us; the launch traced here: 401 us
  waiting for transfers between devices  302 us (75%)
  blocking collectives  55.4 us (14%)
  matrix products  21.9 us (5%)
  between operations  13.9 us (3%)
  other arithmetic  4.9 us (1%)
    reduce_scatter x1, waiting for transfers between devices, on_device(): returned = lax.psum_scatter(spread, 'sub', scatter_dimension=1, tiled=True)  82.2 us
    unnamed x6, waiting for transfers between devices  65.3 us
    psum x1, blocking collectives, on_device(): sums, counts = lax.psum((sums_part, jnp.sum(member, axis=0)), 'sub')  55.4 us
    all_gather x1, waiting for transfers between devices, on_device(): whole = lax.all_gather(blocks, 'sub', axis=1, tiled=True)  54.7 us
    psum x1, waiting for transfers between devices, on_device(): sums, counts = lax.psum((sums_part, jnp.sum(member, axis=0)), 'sub')  52.7 us
    all_gather x1, waiting for transfers between devices, on_device(): coarse_sol = jnp.sum(lax.all_gather(coarse_part, 'sub'), axis=0)  46.7 us
  transfers between devices with their start and end apart: 5, of which 5 were waited for; matrix products, arithmetic and copies ran while one was open for 4% of the time, Pallas kernels for 0%

profile of v1, /device:TPU:2, one launch (start us, length us, event | category | flops | bytes accessed | tf_op | source)
XLA Modules:
  0.0 401.2 jit_solution(14877120524996691215)
XLA Ops:
  6.5 0.0 copy-start
  6.5 0.0 all-reduce.4.cloned.1.call-start
  6.5 1.0 copy.9
  7.5 0.0 copy-start.1
  7.5 1.6 convolution_bitcast_fusion.2
  9.1 0.0 all-reduce.4.cloned.1.call-update
  9.2 0.0 all-gather.5.cloned.1.call-start
  9.2 0.0 copy-done.1
  9.2 0.7 all-gather.5.cloned.1.call-update
  9.9 0.0 all-reduce.6.cloned.1.call-start
  10.0 0.0 copy-done
  10.0 0.2 dynamic-slice_reduce_fusion
  10.2 0.7 convert_reduce_fusion
  10.9 55.4 %psum.15 = f32[64]{0:T(128)S(1)} all-reduce(f32[64]{0:T(128)S(1)} %convert_reduce_fusion), channel_id=1, replica_groups=mesh['grp'=8,'sub'=32] {'sub'}, use_global_device_ids=true, to_apply=%region_4.5 | all-reduce | flops 64 | bytes 512 | tf_op jit(solution)/shard_map/psum | solution.py:51
  66.3 0.9 bitcast_convert_fusion
  67.3 52.7 %all-reduce.4.cloned.1.call-done = f32[2,64,128]{2,1,0:T(8,128)} async-done(((f32[2,64,128]{2,1,0:T(8,128)}), f32[2,64,128]{2,1,0:T(8,128)}) %all-reduce.4.cloned.1.call-update) | async-done | bytes 65552 | tf_op jit(solution)/shard_map/psum | solution.py:51
  120.0 0.9 fusion.22
  120.9 54.7 %all-gather.5.cloned.1.call-done = f32[16,768,128]{2,1,0:T(8,128)} async-done(((f32[16,24,128]{2,1,0:T(8,128)}), f32[16,768,128]{2,1,0:T(8,128)}) %all-gather.5.cloned.1.call-update) | async-done | bytes 6291472 | tf_op jit(solution)/shard_map/all_gather | solution.py:27
  175.7 4.8 %fusion.4 = bf16[16,8,128]{2,1,0:T(8,128)(2,1)S(1)} fusion(f32[16,768,128]{2,1,0:T(8,128)} %all-gather.5.cloned.1.call-done, s32[8]{0:T(128)S(1)} %dynamic-slice_reduce_fusion), kind=kOutput, calls=%fused_computation.8 | convolution fusion | flops 151017472 | bytes 6324256 | tf_op jit(solution)/shard_map/kb,rbc->rkc/dot_general | solution.py:28
  180.5 6.0 %fusion = f32[16,4096]{1,0:T(8,128)} fusion(bf16[1,512,4096]{2,1,0:T(8,128)(2,1)} %param.8, bf16[2,8,32,128]{3,2,1,0:T(8,128)(2,1)S(1)} %bitcast.65), kind=kOutput, calls=%fused_computation.1 | convolution fusion | flops 134225920 | bytes 4587520 | tf_op jit(solution)/shard_map/dot_general | solution.py:37
  186.5 0.0 all-reduce.6.cloned.1.call-update
  186.5 0.0 copy-start.3
  186.6 0.0 copy-start.2
  186.6 0.0 all-gather.7.cloned.1.call-start
  186.6 7.0 %convolution_bitcast_fusion = f32[1,2,8192]{2,1,0:T(2,128)} fusion(bf16[256,8192]{1,0:T(8,128)(2,1)} %param.9, bf16[1,2,64,128]{3,2,1,0:T(8,128)(2,1)S(1)} %fusion.22), kind=kOutput, calls=%fused_computation | convolution fusion | flops 16777728 | bytes 4292608 | tf_op jit(solution)/shard_map/dot_general | solution.py:60
  193.6 0.0 all-gather.7.cloned.1.call-update
  193.6 0.0 reduce-scatter.2.cloned.1.call-start
  193.7 0.0 copy-done.3
  193.7 0.6 dynamic-slice
  194.9 64.5 %all-reduce.6.cloned.1.call-done = f32[16,4096]{1,0:T(8,128)} async-done(((f32[16,4096]{1,0:T(8,128)}), f32[16,4096]{1,0:T(8,128)}) %all-reduce.6.cloned.1.call-update) | async-done | bytes 262160
  259.4 0.9 dynamic-slice_bitcast_fusion
  260.4 1.5 convolution_bitcast_fusion.1
  261.9 0.0 reduce-scatter.2.cloned.1.call-update
  261.9 46.7 %all-gather.7.cloned.1.call-done = f32[32,2,8192]{2,1,0:T(2,128)} async-done(((f32[1,2,8192]{2,1,0:T(2,128)}), f32[32,2,8192]{2,1,0:T(2,128)}) %all-gather.7.cloned.1.call-update) | async-done | bytes 2097168 | tf_op jit(solution)/shard_map/all_gather | solution.py:61
  308.6 2.3 reduce_sum.19
  310.9 82.2 %reduce-scatter.2.cloned.1.call-done = f32[2,24,128]{2,1,0:T(8,128)} async-done(((f32[2,768,128]{2,1,0:T(8,128)}), f32[2,24,128]{2,1,0:T(8,128)}) %reduce-scatter.2.cloned.1.call-update) | async-done | bytes 24592 | tf_op jit(solution)/shard_map/reduce_scatter | solution.py:46
  393.1 0.0 copy-done.2
  393.1 0.9 fusion.11
  394.0 0.6 copy.32
  (3 shorter events, 0.0 us)
Async XLA Ops:
  6.5 3.4 copy-start
  6.5 113.4 %all-reduce.4.cloned.1.call-start = ((), (), s32[]{:S(2)}) async-start(), calls=%async_computation.3 | async-start | bytes 131072 | tf_op jit(solution)/shard_map/psum | solution.py:51
  7.5 1.7 copy-start.1
  9.2 166.5 %all-gather.5.cloned.1.call-start = ((), (), s32[]{:S(2)}) async-start(), calls=%async_computation.1 | async-start | bytes 6488064 | tf_op jit(solution)/shard_map/all_gather | solution.py:27
  9.9 249.5 %all-reduce.6.cloned.1.call-start = ((), (), s32[]{:S(2)}) async-start(), calls=%async_computation.5 | async-start | bytes 524288
  186.5 7.1 %copy-start.3 = (u32[256]{0:T(256)S(1)}, u32[256]{0:T(256)}, u32[]{:S(2)}) copy-start(u32[256]{0:T(256)} %constant.28) | copy-start | bytes 3076
  186.6 206.5 %copy-start.2 = (s32[24]{0:T(128)S(1)}, s32[24]{0:T(128)}, u32[]{:S(2)}) copy-start(s32[24]{0:T(128)} %param.7) | copy-start | bytes 292
  186.6 122.0 %all-gather.7.cloned.1.call-start = ((), (), s32[]{:S(2)}) async-start(), calls=%async_computation.4 | async-start | bytes 2162688 | tf_op jit(solution)/shard_map/all_gather | solution.py:61
  193.6 199.5 %reduce-scatter.2.cloned.1.call-start = ((), (), s32[]{:S(2)}) async-start(), calls=%async_computation.2 | async-start | bytes 811008 | tf_op jit(solution)/shard_map/reduce_scatter | solution.py:46
Sparse Core Ops, SparseCore 0:
  10.6 109.3 all-reduce.3
  122.7 52.9 all-gather.4
  186.7 72.7 all-reduce.5
  261.8 46.7 all-gather.6
  312.2 80.7 reduce-scatter.1
